TPU v7x, 32 devices: a whole 2x2x4 slice. The times are simulated.
32 devices in a mesh: groups: 2 (over y), gx: 4 (over z), gy: 2 (over x), gz: 2 (over core).
Axes of the slice: x: 2, y: 2, z: 4, core: 2. Of those that a mesh axis runs over, the one named last changes fastest.
Arguments:
- log_perm: float32 [32, 32, 1024], P(('groups', 'gx'), 'gy', 'gz'), parts along dimension 0, may hold values from -4 to 4
- source: float32 [32, 32, 1024], P(('groups', 'gx'), 'gy', 'gz'), parts along dimension 0, may hold values from -24 to 24
- low_bound: float32 [1], replicated, may hold values from 0.05 to 0.4
- high_bound: float32 [1], replicated, may hold values from 1.8 to 2.4
Outputs:
- fine_pressure: float32 [32, 32, 1024], P(('groups', 'gx'), 'gy', 'gz'), parts along dimension 0
- difference: float32 [32, 32, 1024], P(('groups', 'gx'), 'gy', 'gz'), parts along dimension 0
There are 2 independent parts, one for each index of `groups`. A program takes and returns all parts, laid end to end along the dimension named above; an argument that names none is the same for every part. Nothing has to cross between parts.
All inputs are finite; a program needn't handle non-finite values.
Results may differ from a plain program's by a relative error of at most 0.00002.
Values sent between devices are 32-bit elements; how exact they have to be, the bound alone decides.
A program may use at most 64 MiB of HBM per device.

v0:
```python
import jax
import jax.numpy as jnp
from jax import lax
from jax.sharding import PartitionSpec as P

DEGREE = 3


storage_rate = 0.1


def extended_2(array, sides, width):
    for axis, dim in sides:
        peers, length = (lax.axis_size(axis), array.shape[dim])
        up = [(i, (i + 1) % peers) for i in range(peers - 1)]
        down = [(j, i) for i, j in up]
        last = lax.slice_in_dim(array, length - width, length, axis=dim)
        leading = lax.slice_in_dim(array, 0, width, axis=dim)
        before = lax.ppermute(last, axis, up)
        after = lax.ppermute(leading, axis, down)
        array = jnp.concatenate([before, array, after], axis=dim)
    return array


def harmonic(first_perm, second_perm, face_scale):
    total = first_perm + second_perm
    inside = total > 0.0
    safe_total = jnp.where(inside, total, 1.0)
    return jnp.where(inside, face_scale * 2.0 * first_perm * second_perm / safe_total, 0.0)


def coefficients(padded, face_scale, storage):
    centre = padded[1:-1, 1:-1, 1:-1]
    east_face = harmonic(centre, padded[2:, 1:-1, 1:-1], face_scale)
    west_face = harmonic(centre, padded[:-2, 1:-1, 1:-1], face_scale)
    north_face = harmonic(centre, padded[1:-1, 2:, 1:-1], face_scale)
    south_face = harmonic(centre, padded[1:-1, :-2, 1:-1], face_scale)
    upper_face = harmonic(centre, padded[1:-1, 1:-1, 2:], face_scale)
    lower_face = harmonic(centre, padded[1:-1, 1:-1, :-2], face_scale)
    diagonal = storage + east_face + west_face + north_face + south_face + upper_face + lower_face
    return (east_face, west_face, north_face, south_face, upper_face, lower_face, diagonal)


def operate(padded, face_terms):
    east_face, west_face, north_face, south_face, upper_face, lower_face, diagonal = face_terms
    centre = padded[1:-1, 1:-1, 1:-1]
    beside = east_face * padded[2:, 1:-1, 1:-1] + west_face * padded[:-2, 1:-1, 1:-1]
    beside = beside + north_face * padded[1:-1, 2:, 1:-1] + south_face * padded[1:-1, :-2, 1:-1]
    beside = beside + upper_face * padded[1:-1, 1:-1, 2:] + lower_face * padded[1:-1, 1:-1, :-2]
    return diagonal * centre - beside


def chebyshev_terms(lower_edge, upper_edge):
    centre_value = (upper_edge + lower_edge) * 0.5
    half_width = (upper_edge - lower_edge) * 0.5
    return (centre_value, half_width, centre_value / half_width)


def chebyshev_levels(
    exchange, padded_perms, sources, face_scales, storages, lower_edge, upper_edge
):
    term_sets = [
        coefficients(padded, scale, storage)
        for padded, scale, storage in zip(padded_perms, face_scales, storages)
    ]
    centre_value, half_width, ratio_sigma = chebyshev_terms(lower_edge, upper_edge)
    rho_now = 1.0 / ratio_sigma
    directions = [
        source_part / (centre_value * face_terms[6])
        for source_part, face_terms in zip(sources, term_sets)
    ]
    solutions = list(directions)
    residuals = list(sources)
    for iteration in range(DEGREE):
        padded_dirs = exchange(tuple(directions))
        rho_next = 1.0 / (2.0 * ratio_sigma - rho_now)
        face_terms = term_sets[0]
        residuals[0] = residuals[0] - operate(padded_dirs[0], face_terms)
        directions[0] = (
            rho_next * rho_now * directions[0]
            + 2.0 * rho_next / half_width * residuals[0] / face_terms[6]
        )
        solutions[0] = solutions[0] + directions[0]
        rho_now = rho_next
    return tuple(solutions)


def crop_one(field):
    return field[1:-1, 1:-1, 1:-1]


def refine(field):
    size_x, size_y, size_z = field.shape
    widened = jnp.broadcast_to(field[:, None, :, None, :, None], (size_x, 2, size_y, 2, size_z, 2))
    return widened.reshape(2 * size_x, 2 * size_y, 2 * size_z)


def coarse_single(fields):
    return (extended_2(fields[0], (("gx", 0), ("gy", 1), ("gz", 2)), 1),)


def deep_extend(layers):
    stacked = jnp.stack(layers)
    return extended_2(stacked, (("gx", 1), ("gy", 2), ("gz", 3)), DEGREE + 1)


def fine_deep(extended, lower_edge, upper_edge):
    face_terms = coefficients(extended[0], 1.0, storage_rate)
    centre_value, half_width, ratio_sigma = chebyshev_terms(lower_edge, upper_edge)
    rho_now = 1.0 / ratio_sigma
    residual = crop_one(extended[1])
    direction = residual / (centre_value * face_terms[6])
    solution = direction
    for iteration in range(DEGREE):
        face_terms = tuple((crop_one(member) for member in face_terms))
        residual = crop_one(residual) - operate(direction, face_terms)
        rho_next = 1.0 / (2.0 * ratio_sigma - rho_now)
        direction = (
            rho_next * rho_now * crop_one(direction)
            + 2.0 * rho_next / half_width * residual / face_terms[6]
        )
        solution = crop_one(solution) + direction
        rho_now = rho_next
    return solution


def shards(log_perm, source, low_bound, high_bound):
    lower_edge = low_bound[0]
    upper_edge = high_bound[0]
    cells_x, cells_y, cells_z = log_perm.shape
    perm_field = jnp.exp(log_perm)
    blocks = (cells_x // 2, 2, cells_y // 2, 2, cells_z // 2, 2)
    coarse_perm = jnp.exp(log_perm.reshape(blocks).mean(axis=(1, 3, 5)))
    coarse_source = source.reshape(blocks).sum(axis=(1, 3, 5))
    coarse_storage = 8.0 * storage_rate
    fine = fine_deep(deep_extend((perm_field, source)), lower_edge, upper_edge)
    coarse = chebyshev_levels(
        coarse_single,
        coarse_single((coarse_perm,)),
        (coarse_source,),
        (2.0,),
        (coarse_storage,),
        lower_edge,
        upper_edge,
    )[0]
    spread = refine(coarse)
    return (fine, fine - spread)


def solution(mesh):
    return jax.shard_map(
        shards,
        mesh=mesh,
        in_specs=(P(("groups", "gx"), "gy", "gz"), P(("groups", "gx"), "gy", "gz"), P(), P()),
        out_specs=(P(("groups", "gx"), "gy", "gz"), P(("groups", "gx"), "gy", "gz")),
        check_vma=False,
    )
```

profile of v0, /device:TPU:0, one launch (start us, length us, event | category | flops | bytes accessed | tf_op | source)
XLA Modules:
  0.0 140.4 jit_solution(17191093065461808956)
XLA Ops:
  0.6 10.5 %reshape.21 = f32[2,2,8,2,256,2]{5,4,3,2,1,0:T(8,128)} reshape(f32[4,16,512]{2,1,0:T(8,128)} %param.4) | data formatting | bytes 262144 | tf_op jit(solution)/shard_map/reshape | solution.py:133
  11.2 4.1 %reduce_sum.19 = f32[2,8,256]{2,1,0:T(8,128)S(1)} reduce(f32[2,2,8,2,256,2]{5,4,3,2,1,0:T(8,128)} %reshape.21, f32[]{:T(128)} %constant.9.clone.1), dimensions={1,3,5}, to_apply=%region_1.0 | reduce | flops 28672 | bytes 147460 | tf_op jit(solution)/shard_map/reduce_sum | solution.py:133
  16.6 5.6 %collective-permute-start.7 = (f32[1,8,256]{2,1,0:T(8,128)S(1)}, f32[1,8,256]{2,1,0:T(8,128)S(1)}, u32[]{:S(2)}, u32[]{:S(2)}) collective-permute-start(f32[1,8,256]{2,1,0:T(8,128)S(1)} %get-tuple-element.52), channel_id=1, source_target_pairs={{0,4},{4,8},{8,12},{1,5},{5,9},{9,13},{2,6},{6,10},{10,14},{3,7},{... | collective-permute-start | bytes 24584 | tf_op jit(solution)/shard_map/ppermute | solution.py:19
  24.8 4.5 %collective-permute-start.9 = (f32[4,1,256]{2,1,0:T(1,128)S(1)}, f32[4,1,256]{2,1,0:T(1,128)S(1)}, u32[]{:S(2)}, u32[]{:S(2)}) collective-permute-start(f32[4,1,256]{2,1,0:T(1,128)S(1)} %get-tuple-element.44), channel_id=1, source_target_pairs={{0,2},{1,3},{4,6},{5,7},{8,10},{9,11},{12,14},{13,15},{16,18},{17,... | collective-permute-start | bytes 12296 | tf_op jit(solution)/shard_map/ppermute | solution.py:19
  29.4 9.8 %reshape.20 = f32[2,2,8,2,256,2]{5,4,3,2,1,0:T(8,128)} reshape(f32[4,16,512]{2,1,0:T(8,128)S(1)} %copy-done) | data formatting | bytes 262144 | tf_op jit(solution)/shard_map/reshape | solution.py:134
  39.2 4.1 %reduce_sum.18 = f32[2,8,256]{2,1,0:T(8,128)S(1)} reduce(f32[2,2,8,2,256,2]{5,4,3,2,1,0:T(8,128)} %reshape.20, f32[]{:T(128)} %constant.9.clone.1), dimensions={1,3,5}, to_apply=%region_0.0 | reduce | flops 28672 | bytes 147460 | tf_op jit(solution)/shard_map/reduce_sum | solution.py:134
  45.9 3.0 %collective-permute-start.11 = (f32[4,10,1]{2,1,0:T(8,128)S(1)}, f32[4,10,1]{2,1,0:T(8,128)S(1)}, u32[]{:S(2)}, u32[]{:S(2)}) collective-permute-start(f32[4,10,1]{2,1,0:T(8,128)S(1)} %get-tuple-element.36), channel_id=1, source_target_pairs={{0,1},{2,3},{4,5},{6,7},{8,9},{10,11},{12,13},{14,15},{16,17},{18,... | collective-permute-start | bytes 488 | tf_op jit(solution)/shard_map/ppermute | solution.py:19
  51.2 4.8 %collective-permute-start.13 = (f32[1,8,256]{2,1,0:T(8,128)S(1)}, f32[1,8,256]{2,1,0:T(8,128)S(1)}, u32[]{:S(2)}, u32[]{:S(2)}) collective-permute-start(f32[1,8,256]{2,1,0:T(8,128)S(1)} %get-tuple-element.50), channel_id=1, source_target_pairs={{0,4},{4,8},{8,12},{1,5},{5,9},{9,13},{2,6},{6,10},{10,14},{3,7},{... | collective-permute-start | bytes 24584 | tf_op jit(solution)/shard_map/ppermute | solution.py:19
  58.7 4.5 %collective-permute-start.15 = (f32[4,1,256]{2,1,0:T(1,128)S(1)}, f32[4,1,256]{2,1,0:T(1,128)S(1)}, u32[]{:S(2)}, u32[]{:S(2)}) collective-permute-start(f32[4,1,256]{2,1,0:T(1,128)S(1)} %get-tuple-element.42), channel_id=1, source_target_pairs={{0,2},{1,3},{4,6},{5,7},{8,10},{9,11},{12,14},{13,15},{16,18},{17,... | collective-permute-start | bytes 12296 | tf_op jit(solution)/shard_map/ppermute | solution.py:19
  67.3 1.7 %collective-permute-done.16 = f32[4,10,1]{2,1,0:T(8,128)S(1)} collective-permute-done((f32[4,10,1]{2,1,0:T(8,128)S(1)}, f32[4,10,1]{2,1,0:T(8,128)S(1)}, u32[]{:S(2)}, u32[]{:S(2)}) %collective-permute-start.16) | collective-permute-done | bytes 192 | tf_op jit(solution)/shard_map/ppermute | solution.py:20
  70.5 4.8 %collective-permute-start.19 = (f32[1,8,256]{2,1,0:T(8,128)S(1)}, f32[1,8,256]{2,1,0:T(8,128)S(1)}, u32[]{:S(2)}, u32[]{:S(2)}) collective-permute-start(f32[1,8,256]{2,1,0:T(8,128)S(1)} %get-tuple-element.48), channel_id=1, source_target_pairs={{0,4},{4,8},{8,12},{1,5},{5,9},{9,13},{2,6},{6,10},{10,14},{3,7},{... | collective-permute-start | bytes 24584 | tf_op jit(solution)/shard_map/ppermute | solution.py:19
  77.9 4.5 %collective-permute-start.21 = (f32[4,1,256]{2,1,0:T(1,128)S(1)}, f32[4,1,256]{2,1,0:T(1,128)S(1)}, u32[]{:S(2)}, u32[]{:S(2)}) collective-permute-start(f32[4,1,256]{2,1,0:T(1,128)S(1)} %get-tuple-element.40), channel_id=1, source_target_pairs={{0,2},{1,3},{4,6},{5,7},{8,10},{9,11},{12,14},{13,15},{16,18},{17,... | collective-permute-start | bytes 12296 | tf_op jit(solution)/shard_map/ppermute | solution.py:19
  83.8 4.8 %collective-permute-start = (f32[2,4,16,512]{3,2,1,0:T(8,128)S(1)}, f32[2,4,16,512]{3,2,1,0:T(8,128)S(1)}, u32[]{:S(2)}, u32[]{:S(2)}) collective-permute-start(f32[2,4,16,512]{3,2,1,0:T(8,128)S(1)} %pad_maximum_fusion.7), channel_id=1, source_target_pairs={{0,4},{4,8},{8,12},{1,5},{5,9},{9,13},{2,6},{6,10},{10,14},{3,7},{... | collective-permute-start | bytes 786440 | tf_op jit(solution)/shard_map/ppermute | solution.py:19
  91.5 1.7 %collective-permute-done.22 = f32[4,10,1]{2,1,0:T(8,128)S(1)} collective-permute-done((f32[4,10,1]{2,1,0:T(8,128)S(1)}, f32[4,10,1]{2,1,0:T(8,128)S(1)}, u32[]{:S(2)}, u32[]{:S(2)}) %collective-permute-start.22) | collective-permute-done | bytes 192 | tf_op jit(solution)/shard_map/ppermute | solution.py:20
  94.6 4.5 %collective-permute-start.25 = (f32[1,8,256]{2,1,0:T(8,128)S(1)}, f32[1,8,256]{2,1,0:T(8,128)S(1)}, u32[]{:S(2)}, u32[]{:S(2)}) collective-permute-start(f32[1,8,256]{2,1,0:T(8,128)S(1)} %get-tuple-element.46), channel_id=1, source_target_pairs={{0,4},{4,8},{8,12},{1,5},{5,9},{9,13},{2,6},{6,10},{10,14},{3,7},{... | collective-permute-start | bytes 24584 | tf_op jit(solution)/shard_map/ppermute | solution.py:19
  101.8 4.5 %collective-permute-start.27 = (f32[4,1,256]{2,1,0:T(1,128)S(1)}, f32[4,1,256]{2,1,0:T(1,128)S(1)}, u32[]{:S(2)}, u32[]{:S(2)}) collective-permute-start(f32[4,1,256]{2,1,0:T(1,128)S(1)} %get-tuple-element.38), channel_id=1, source_target_pairs={{0,2},{1,3},{4,6},{5,7},{8,10},{9,11},{12,14},{13,15},{16,18},{17,... | collective-permute-start | bytes 12296 | tf_op jit(solution)/shard_map/ppermute | solution.py:19
  109.1 4.6 %collective-permute-start.2 = (f32[2,12,4,512]{3,2,1,0:T(4,128)S(1)}, f32[2,12,4,512]{3,2,1,0:T(4,128)S(1)}, u32[]{:S(2)}, u32[]{:S(2)}) collective-permute-start(f32[2,12,4,512]{3,2,1,0:T(4,128)S(1)} %get-tuple-element.27), channel_id=1, source_target_pairs={{0,2},{1,3},{4,6},{5,7},{8,10},{9,11},{12,14},{13,15},{16,18},{17,... | collective-permute-start | bytes 589832 | tf_op jit(solution)/shard_map/ppermute | solution.py:19
  118.3 3.2 %collective-permute-start.4 = (f32[2,12,24,4]{3,2,1,0:T(8,128)S(1)}, f32[2,12,24,4]{3,2,1,0:T(8,128)S(1)}, u32[]{:S(2)}, u32[]{:S(2)}) collective-permute-start(f32[2,12,24,4]{3,2,1,0:T(8,128)S(1)} %get-tuple-element.25), channel_id=1, source_target_pairs={{0,1},{2,3},{4,5},{6,7},{8,9},{10,11},{12,13},{14,15},{16,17},{18,... | collective-permute-start | bytes 27656 | tf_op jit(solution)/shard_map/ppermute | solution.py:19
  121.7 3.8 %broadcast_in_dim.38 = f32[2,2,8,2,256,2]{5,4,3,2,1,0:T(8,128)} broadcast(f32[2,8,256]{2,1,0:T(8,128)S(1)} %fusion.45), dimensions={0,2,4} | broadcast | bytes 147456 | tf_op jit(solution)/shard_map/broadcast_in_dim | solution.py:94
  125.6 6.9 %reshape.22 = f32[4,16,512]{2,1,0:T(8,128)S(1)} reshape(f32[2,2,8,2,256,2]{5,4,3,2,1,0:T(8,128)} %broadcast_in_dim.38) | data formatting | bytes 262144 | tf_op jit(solution)/shard_map/reshape | solution.py:95
  133.5 1.5 %slice_divide_fusion = (f32[10,22,518]{2,1,0:T(8,128)S(1)}, f32[10,22,518]{2,1,0:T(8,128)S(1)}, f32[10,22,518]{2,1,0:T(8,128)S(1)}, f32[10,22,518]{2,1,0:T(8,128...) fusion(f32[12,24,520]{2,1,0:T(8,128)S(1)} %get-tuple-element.24, ...), kind=kLoop, calls=%fused_computation.21 | loop fusion | flops 5128200 | bytes 7293444 | tf_op jit(solution)/shard_map/div | solution.py:112
  135.2 2.2 %divide_add_fusion = (f32[8,20,516]{2,1,0:T(8,128)S(1)}, f32[8,20,516]{2,1,0:T(8,128)S(1)}) fusion(f32[10,22,518]{2,1,0:T(8,128)S(1)} %get-tuple-element.16, f32[]{:T(128)S(6)} %div.108, f32[]{:T(128)S(6)} %mul.321, f32[10,22,518]{2,1,0:T(8,128)S(1)} %get-tuple-element.15, f32[10,22,518]{2,1,0:T(8,128)S(1)} %get-tuple-element.22, ...), kind=kLoop, calls=%fused_computation.36 | loop fusion | flops 1486080 | bytes 5614088 | tf_op jit(solution)/shard_map/add | solution.py:119
  137.4 1.6 %divide_add_fusion.1 = (f32[6,18,514]{2,1,0:T(8,128)S(1)}, f32[6,18,514]{2,1,0:T(8,128)S(1)}, f32[6,18,514]{2,1,0:T(8,128)S(1)}) fusion(f32[10,22,518]{2,1,0:T(8,128)S(1)} %get-tuple-element.16, f32[]{:T(128)S(6)} %div.111, f32[]{:T(128)S(6)} %mul.334, f32[8,20,516]{2,1,0:T(8,128)S(1)} %get-tuple-element.13, f32[10,22,518]{2,1,0:T(8,128)S(1)} %get-tuple-element.22, ...), kind=kLoop, calls=%fused_computation.50 | loop fusion | flops 999216 | bytes 3996872 | tf_op jit(solution)/shard_map/add | solution.py:119
  139.0 1.4 fusion.85
  (78 shorter events, 34.5 us)
Async XLA Ops:
  15.3 6.9 %collective-permute-start.6 = (f32[1,8,256]{2,1,0:T(8,128)S(1)}, f32[1,8,256]{2,1,0:T(8,128)S(1)}, u32[]{:S(2)}, u32[]{:S(2)}) collective-permute-start(f32[1,8,256]{2,1,0:T(8,128)S(1)} %get-tuple-element.53), channel_id=1, source_target_pairs={{4,0},{8,4},{12,8},{5,1},{9,5},{13,9},{6,2},{10,6},{14,10},{7,3},{... | collective-permute-start | bytes 24584 | tf_op jit(solution)/shard_map/ppermute | solution.py:20
  16.6 6.9 %collective-permute-start.7 = (f32[1,8,256]{2,1,0:T(8,128)S(1)}, f32[1,8,256]{2,1,0:T(8,128)S(1)}, u32[]{:S(2)}, u32[]{:S(2)}) collective-permute-start(f32[1,8,256]{2,1,0:T(8,128)S(1)} %get-tuple-element.52), channel_id=1, source_target_pairs={{0,4},{4,8},{8,12},{1,5},{5,9},{9,13},{2,6},{6,10},{10,14},{3,7},{... | collective-permute-start | bytes 24584 | tf_op jit(solution)/shard_map/ppermute | solution.py:19
  23.5 21.0 %collective-permute-start.8 = (f32[4,1,256]{2,1,0:T(1,128)S(1)}, f32[4,1,256]{2,1,0:T(1,128)S(1)}, u32[]{:S(2)}, u32[]{:S(2)}) collective-permute-start(f32[4,1,256]{2,1,0:T(1,128)S(1)} %get-tuple-element.45), channel_id=1, source_target_pairs={{2,0},{3,1},{6,4},{7,5},{10,8},{11,9},{14,12},{15,13},{18,16},{19,... | collective-permute-start | bytes 12296 | tf_op jit(solution)/shard_map/ppermute | solution.py:20
  24.8 19.7 %collective-permute-start.9 = (f32[4,1,256]{2,1,0:T(1,128)S(1)}, f32[4,1,256]{2,1,0:T(1,128)S(1)}, u32[]{:S(2)}, u32[]{:S(2)}) collective-permute-start(f32[4,1,256]{2,1,0:T(1,128)S(1)} %get-tuple-element.44), channel_id=1, source_target_pairs={{0,2},{1,3},{4,6},{5,7},{8,10},{9,11},{12,14},{13,15},{16,18},{17,... | collective-permute-start | bytes 12296 | tf_op jit(solution)/shard_map/ppermute | solution.py:19
  49.9 6.1 %collective-permute-start.12 = (f32[1,8,256]{2,1,0:T(8,128)S(1)}, f32[1,8,256]{2,1,0:T(8,128)S(1)}, u32[]{:S(2)}, u32[]{:S(2)}) collective-permute-start(f32[1,8,256]{2,1,0:T(8,128)S(1)} %get-tuple-element.51), channel_id=1, source_target_pairs={{4,0},{8,4},{12,8},{5,1},{9,5},{13,9},{6,2},{10,6},{14,10},{7,3},{... | collective-permute-start | bytes 24584 | tf_op jit(solution)/shard_map/ppermute | solution.py:20
  51.2 6.2 %collective-permute-start.13 = (f32[1,8,256]{2,1,0:T(8,128)S(1)}, f32[1,8,256]{2,1,0:T(8,128)S(1)}, u32[]{:S(2)}, u32[]{:S(2)}) collective-permute-start(f32[1,8,256]{2,1,0:T(8,128)S(1)} %get-tuple-element.50), channel_id=1, source_target_pairs={{0,4},{4,8},{8,12},{1,5},{5,9},{9,13},{2,6},{6,10},{10,14},{3,7},{... | collective-permute-start | bytes 24584 | tf_op jit(solution)/shard_map/ppermute | solution.py:19
  57.4 6.0 %collective-permute-start.14 = (f32[4,1,256]{2,1,0:T(1,128)S(1)}, f32[4,1,256]{2,1,0:T(1,128)S(1)}, u32[]{:S(2)}, u32[]{:S(2)}) collective-permute-start(f32[4,1,256]{2,1,0:T(1,128)S(1)} %get-tuple-element.43), channel_id=1, source_target_pairs={{2,0},{3,1},{6,4},{7,5},{10,8},{11,9},{14,12},{15,13},{18,16},{19,... | collective-permute-start | bytes 12296 | tf_op jit(solution)/shard_map/ppermute | solution.py:20
  58.7 5.9 %collective-permute-start.15 = (f32[4,1,256]{2,1,0:T(1,128)S(1)}, f32[4,1,256]{2,1,0:T(1,128)S(1)}, u32[]{:S(2)}, u32[]{:S(2)}) collective-permute-start(f32[4,1,256]{2,1,0:T(1,128)S(1)} %get-tuple-element.42), channel_id=1, source_target_pairs={{0,2},{1,3},{4,6},{5,7},{8,10},{9,11},{12,14},{13,15},{16,18},{17,... | collective-permute-start | bytes 12296 | tf_op jit(solution)/shard_map/ppermute | solution.py:19
  69.2 6.2 %collective-permute-start.18 = (f32[1,8,256]{2,1,0:T(8,128)S(1)}, f32[1,8,256]{2,1,0:T(8,128)S(1)}, u32[]{:S(2)}, u32[]{:S(2)}) collective-permute-start(f32[1,8,256]{2,1,0:T(8,128)S(1)} %get-tuple-element.49), channel_id=1, source_target_pairs={{4,0},{8,4},{12,8},{5,1},{9,5},{13,9},{6,2},{10,6},{14,10},{7,3},{... | collective-permute-start | bytes 24584 | tf_op jit(solution)/shard_map/ppermute | solution.py:20
  70.5 6.2 %collective-permute-start.19 = (f32[1,8,256]{2,1,0:T(8,128)S(1)}, f32[1,8,256]{2,1,0:T(8,128)S(1)}, u32[]{:S(2)}, u32[]{:S(2)}) collective-permute-start(f32[1,8,256]{2,1,0:T(8,128)S(1)} %get-tuple-element.48), channel_id=1, source_target_pairs={{0,4},{4,8},{8,12},{1,5},{5,9},{9,13},{2,6},{6,10},{10,14},{3,7},{... | collective-permute-start | bytes 24584 | tf_op jit(solution)/shard_map/ppermute | solution.py:19
  76.7 12.1 %collective-permute-start.20 = (f32[4,1,256]{2,1,0:T(1,128)S(1)}, f32[4,1,256]{2,1,0:T(1,128)S(1)}, u32[]{:S(2)}, u32[]{:S(2)}) collective-permute-start(f32[4,1,256]{2,1,0:T(1,128)S(1)} %get-tuple-element.41), channel_id=1, source_target_pairs={{2,0},{3,1},{6,4},{7,5},{10,8},{11,9},{14,12},{15,13},{18,16},{19,... | collective-permute-start | bytes 12296 | tf_op jit(solution)/shard_map/ppermute | solution.py:20
  77.9 10.8 %collective-permute-start.21 = (f32[4,1,256]{2,1,0:T(1,128)S(1)}, f32[4,1,256]{2,1,0:T(1,128)S(1)}, u32[]{:S(2)}, u32[]{:S(2)}) collective-permute-start(f32[4,1,256]{2,1,0:T(1,128)S(1)} %get-tuple-element.40), channel_id=1, source_target_pairs={{0,2},{1,3},{4,6},{5,7},{8,10},{9,11},{12,14},{13,15},{16,18},{17,... | collective-permute-start | bytes 12296 | tf_op jit(solution)/shard_map/ppermute | solution.py:19
  82.5 25.2 %collective-permute-start.1 = (f32[2,4,16,512]{3,2,1,0:T(8,128)S(1)}, f32[2,4,16,512]{3,2,1,0:T(8,128)S(1)}, u32[]{:S(2)}, u32[]{:S(2)}) collective-permute-start(f32[2,4,16,512]{3,2,1,0:T(8,128)S(1)} %pad_maximum_fusion.7), channel_id=1, source_target_pairs={{4,0},{8,4},{12,8},{5,1},{9,5},{13,9},{6,2},{10,6},{14,10},{7,3},{... | collective-permute-start | bytes 786440 | tf_op jit(solution)/shard_map/ppermute | solution.py:20
  83.8 23.9 %collective-permute-start = (f32[2,4,16,512]{3,2,1,0:T(8,128)S(1)}, f32[2,4,16,512]{3,2,1,0:T(8,128)S(1)}, u32[]{:S(2)}, u32[]{:S(2)}) collective-permute-start(f32[2,4,16,512]{3,2,1,0:T(8,128)S(1)} %pad_maximum_fusion.7), channel_id=1, source_target_pairs={{0,4},{4,8},{8,12},{1,5},{5,9},{9,13},{2,6},{6,10},{10,14},{3,7},{... | collective-permute-start | bytes 786440 | tf_op jit(solution)/shard_map/ppermute | solution.py:19
  93.3 5.9 %collective-permute-start.24 = (f32[1,8,256]{2,1,0:T(8,128)S(1)}, f32[1,8,256]{2,1,0:T(8,128)S(1)}, u32[]{:S(2)}, u32[]{:S(2)}) collective-permute-start(f32[1,8,256]{2,1,0:T(8,128)S(1)} %get-tuple-element.47), channel_id=1, source_target_pairs={{4,0},{8,4},{12,8},{5,1},{9,5},{13,9},{6,2},{10,6},{14,10},{7,3},{... | collective-permute-start | bytes 24584 | tf_op jit(solution)/shard_map/ppermute | solution.py:20
  94.6 5.9 %collective-permute-start.25 = (f32[1,8,256]{2,1,0:T(8,128)S(1)}, f32[1,8,256]{2,1,0:T(8,128)S(1)}, u32[]{:S(2)}, u32[]{:S(2)}) collective-permute-start(f32[1,8,256]{2,1,0:T(8,128)S(1)} %get-tuple-element.46), channel_id=1, source_target_pairs={{0,4},{4,8},{8,12},{1,5},{5,9},{9,13},{2,6},{6,10},{10,14},{3,7},{... | collective-permute-start | bytes 24584 | tf_op jit(solution)/shard_map/ppermute | solution.py:19
  100.5 5.9 %collective-permute-start.26 = (f32[4,1,256]{2,1,0:T(1,128)S(1)}, f32[4,1,256]{2,1,0:T(1,128)S(1)}, u32[]{:S(2)}, u32[]{:S(2)}) collective-permute-start(f32[4,1,256]{2,1,0:T(1,128)S(1)} %get-tuple-element.39), channel_id=1, source_target_pairs={{2,0},{3,1},{6,4},{7,5},{10,8},{11,9},{14,12},{15,13},{18,16},{19,... | collective-permute-start | bytes 12296 | tf_op jit(solution)/shard_map/ppermute | solution.py:20
  101.8 5.9 %collective-permute-start.27 = (f32[4,1,256]{2,1,0:T(1,128)S(1)}, f32[4,1,256]{2,1,0:T(1,128)S(1)}, u32[]{:S(2)}, u32[]{:S(2)}) collective-permute-start(f32[4,1,256]{2,1,0:T(1,128)S(1)} %get-tuple-element.38), channel_id=1, source_target_pairs={{0,2},{1,3},{4,6},{5,7},{8,10},{9,11},{12,14},{13,15},{16,18},{17,... | collective-permute-start | bytes 12296 | tf_op jit(solution)/shard_map/ppermute | solution.py:19
  107.8 8.5 %collective-permute-start.3 = (f32[2,12,4,512]{3,2,1,0:T(4,128)S(1)}, f32[2,12,4,512]{3,2,1,0:T(4,128)S(1)}, u32[]{:S(2)}, u32[]{:S(2)}) collective-permute-start(f32[2,12,4,512]{3,2,1,0:T(4,128)S(1)} %get-tuple-element.28), channel_id=1, source_target_pairs={{2,0},{3,1},{6,4},{7,5},{10,8},{11,9},{14,12},{15,13},{18,16},{19,... | collective-permute-start | bytes 589832 | tf_op jit(solution)/shard_map/ppermute | solution.py:20
  109.1 7.7 %collective-permute-start.2 = (f32[2,12,4,512]{3,2,1,0:T(4,128)S(1)}, f32[2,12,4,512]{3,2,1,0:T(4,128)S(1)}, u32[]{:S(2)}, u32[]{:S(2)}) collective-permute-start(f32[2,12,4,512]{3,2,1,0:T(4,128)S(1)} %get-tuple-element.27), channel_id=1, source_target_pairs={{0,2},{1,3},{4,6},{5,7},{8,10},{9,11},{12,14},{13,15},{16,18},{17,... | collective-permute-start | bytes 589832 | tf_op jit(solution)/shard_map/ppermute | solution.py:19
  113.8 7.8 %collective-permute-start.29 = (f32[4,10,1]{2,1,0:T(8,128)S(1)}, f32[4,10,1]{2,1,0:T(8,128)S(1)}, u32[]{:S(2)}, u32[]{:S(2)}) collective-permute-start(f32[4,10,1]{2,1,0:T(8,128)S(1)} %get-tuple-element.31), channel_id=1, source_target_pairs={{0,1},{2,3},{4,5},{6,7},{8,9},{10,11},{12,13},{14,15},{16,17},{18,... | collective-permute-start | bytes 488 | tf_op jit(solution)/shard_map/ppermute | solution.py:19
  115.1 6.6 %collective-permute-start.28 = (f32[4,10,1]{2,1,0:T(8,128)S(1)}, f32[4,10,1]{2,1,0:T(8,128)S(1)}, u32[]{:S(2)}, u32[]{:S(2)}) collective-permute-start(f32[4,10,1]{2,1,0:T(8,128)S(1)} %get-tuple-element.30), channel_id=1, source_target_pairs={{1,0},{3,2},{5,4},{7,6},{9,8},{11,10},{13,12},{15,14},{17,16},{19,... | collective-permute-start | bytes 488 | tf_op jit(solution)/shard_map/ppermute | solution.py:20
  117.0 15.5 %collective-permute-start.5 = (f32[2,12,24,4]{3,2,1,0:T(8,128)S(1)}, f32[2,12,24,4]{3,2,1,0:T(8,128)S(1)}, u32[]{:S(2)}, u32[]{:S(2)}) collective-permute-start(f32[2,12,24,4]{3,2,1,0:T(8,128)S(1)} %get-tuple-element.26), channel_id=1, source_target_pairs={{1,0},{3,2},{5,4},{7,6},{9,8},{11,10},{13,12},{15,14},{17,16},{19,... | collective-permute-start | bytes 27656 | tf_op jit(solution)/shard_map/ppermute | solution.py:20
  118.3 14.2 %collective-permute-start.4 = (f32[2,12,24,4]{3,2,1,0:T(8,128)S(1)}, f32[2,12,24,4]{3,2,1,0:T(8,128)S(1)}, u32[]{:S(2)}, u32[]{:S(2)}) collective-permute-start(f32[2,12,24,4]{3,2,1,0:T(8,128)S(1)} %get-tuple-element.25), channel_id=1, source_target_pairs={{0,1},{2,3},{4,5},{6,7},{8,9},{10,11},{12,13},{14,15},{16,17},{18,... | collective-permute-start | bytes 27656 | tf_op jit(solution)/shard_map/ppermute | solution.py:19
  (8 other events, 74.0 us)
where the time goes:
time: 143 us; the launch traced here: 140 us
  starting transfers between devices  76.8 us (54%)
  local copies, waits for them, and re-layouts  31.7 us (22%)
  other arithmetic  16.5 us (12%)
  waiting for transfers between devices  12.5 us (9%)
  between operations  2.84 us (2%)
    ppermute x15, starting transfers between devices, extended_2(): before = lax.ppermute(last, axis, up)  57.5 us
    ppermute x15, starting transfers between devices, extended_2(): after = lax.ppermute(leading, axis, down)  19.3 us
    reshape x1, local copies, waits for them, and re-layouts, shards(): coarse_perm = jnp.exp(log_perm.reshape(blocks).mean(axis=(1, 3, 5)))  10.5 us
    reshape x1, local copies, waits for them, and re-layouts, shards(): coarse_source = source.reshape(blocks).sum(axis=(1, 3, 5))  9.8 us
    ppermute x15, waiting for transfers between devices, extended_2(): before = lax.ppermute(last, axis, up)  9.02 us
    reshape x1, local copies, waits for them, and re-layouts, refine(): return widened.reshape(2 * size_x, 2 * size_y, 2 * size_z)  6.94 us
    reduce_sum x1, other arithmetic, shards(): coarse_perm = jnp.exp(log_perm.reshape(blocks).mean(axis=(1, 3, 5)))  4.06 us
    reduce_sum x1, other arithmetic, shards(): coarse_source = source.reshape(blocks).sum(axis=(1, 3, 5))  4.06 us
  transfers between devices with their start and end apart: 30, of which 10 were waited for; matrix products, arithmetic and copies ran while one was open for 18% of the time, Pallas kernels for 0%

commit v1 on v0

v1 whole, which is shorter than its diff:
```python
import functools

import jax
import jax.numpy as jnp
from jax import lax
from jax.experimental import pallas as pl
from jax.experimental.pallas import tpu as pltpu
from jax.sharding import PartitionSpec as P

DEGREE = 3
STORAGE = 0.1
LANES = 128
ROWS = 8
MESH = pl.DeviceIdType.MESH
AXES = ("gx", "gy", "gz")


def roll(a, shift, axis):
    return pltpu.roll(a, shift % a.shape[axis], axis)


def iota(shape, axis):
    return lax.broadcasted_iota(jnp.int32, shape, axis)


def even(shape, axis):
    return iota(shape, axis) % 2 == 0


def pair_sum(a, axis):
    return a + jnp.where(even(a.shape, axis), roll(a, -1, axis), roll(a, 1, axis))


def pooled(a, b):
    return pair_sum(pair_sum(a + b, 0), 1)


def packed(a):
    rows, lanes = a.shape[0] // 2, a.shape[1] // 2
    a = jnp.where(even((a.shape[0], lanes), 1), a[:, :lanes], a[:, lanes:])
    return jnp.where(even((rows, lanes), 0), a[:rows], a[rows:])


def unpacked(a):
    for axis in (0, 1):
        is_even = even(a.shape, axis)
        first = jnp.where(is_even, a, roll(a, 1, axis))
        second = jnp.where(is_even, roll(a, -1, axis), a)
        a = jnp.concatenate([first, second], axis=axis)
    return a


def kernel(sizes, low_ref, high_ref, log_hbm, src_hbm, fine_hbm, diff_hbm,
           log_ref, src_ref, fine_ref, diff_ref,
           dirs, face_c, face_y, halo_x, halo_c, halo_y, halo_z,
           inv_k, t_x, t_y, t_z, b_x, b_y, b_z, inv_d, res, sol,
           io_sem, send_sem, recv_sem):
    nx, ny, nz = log_ref.shape
    nc = nx // 2
    nl = nx + nc
    me = {axis: lax.axis_index(axis) for axis in AXES}
    has = {axis: (me[axis] > 0, me[axis] < sizes[axis] - 1) for axis in AXES}

    log_in = pltpu.make_async_copy(log_hbm, log_ref, io_sem.at[0])
    src_in = pltpu.make_async_copy(src_hbm, src_ref, io_sem.at[1])
    log_in.start()
    src_in.start()

    for halo in (halo_x, halo_c, halo_y, halo_z):
        halo[...] = jnp.zeros_like(halo)

    barrier = pltpu.get_barrier_semaphore()
    count = 0
    for axis in AXES:
        for side, step in ((0, -1), (1, 1)):
            if sizes[axis] > 1:
                @pl.when(has[axis][side])
                def _():
                    pl.semaphore_signal(barrier, inc=1, device_id={axis: me[axis] + step},
                                        device_id_type=MESH)
            count = count + has[axis][side].astype(jnp.int32)
    pl.semaphore_wait(barrier, count)

    def faces(turn, kind):
        if kind == 0:
            if turn == 0:
                return "gx", (lambda s: log_hbm.at[s * (nx - 1)]), (lambda s: halo_x.at[turn, s])
            return "gx", (lambda s: dirs.at[turn, s * (nx - 1)]), (lambda s: halo_x.at[turn, s])
        if kind == 1:
            return "gx", (lambda s: face_c.at[turn, s]), (lambda s: halo_c.at[turn, s])
        if kind == 2:
            return "gy", (lambda s: face_y.at[turn, s]), (lambda s: halo_y.at[turn, s])

        def lanes_of(s):
            start = s * (nz - LANES)
            if not isinstance(start, int):
                start = pl.multiple_of(start, LANES)
            return dirs.at[turn, :, :, pl.ds(start, LANES)]

        return "gz", lanes_of, (lambda s: halo_z.at[turn, s])

    def each(turn, kind, outgoing, act):
        axis, source_of, target_of = faces(turn, kind)
        n, here = sizes[axis], me[axis]
        if n == 1:
            return
        if n == 2:
            act(pltpu.make_async_remote_copy(
                src_ref=source_of(1 - here), dst_ref=target_of(here),
                send_sem=send_sem.at[turn, kind, 0], recv_sem=recv_sem.at[turn, kind, 0],
                device_id={axis: 1 - here}, device_id_type=MESH))
            return
        for side, step in ((0, -1), (1, 1)):
            there = 1 - side if outgoing else side

            @pl.when(has[axis][side])
            def _():
                act(pltpu.make_async_remote_copy(
                    src_ref=source_of(side), dst_ref=target_of(there),
                    send_sem=send_sem.at[turn, kind, side],
                    recv_sem=recv_sem.at[turn, kind, there],
                    device_id={axis: here + step}, device_id_type=MESH))

    def start(turn, kind):
        each(turn, kind, True, lambda copy: copy.start())

    def arrive(turn, kind):
        each(turn, kind, False, lambda copy: copy.wait_recv())

    def drain(turn, kind):
        each(turn, kind, True, lambda copy: copy.wait_send())

    start(0, 0)
    log_in.wait()

    def put(turn, i, value):
        dirs[turn, i] = value
        face_y[turn, 0, i:i + 1, :] = value[0:1, :]
        face_y[turn, 1, i:i + 1, :] = value[ny - 1:ny, :]
        if i >= nx and (i == nx or i == nl - 1):
            pack = packed(value)
            if i == nx:
                face_c[turn, 0] = pack
            if i == nl - 1:
                face_c[turn, 1] = pack

    def level(i):
        return (1, 1.0, STORAGE) if i < nx else (2, 2.0, 8.0 * STORAGE)

    order = [nx, nl - 1] + list(range(nx + 1, nl - 1)) + [0, nx - 1] + list(range(1, nx - 1))
    order = list(dict.fromkeys(order))
    for i in order:
        if i < nx:
            put(0, i, log_ref[i])
        else:
            j = 2 * (i - nx)
            put(0, i, pooled(log_ref[j], log_ref[j + 1]) * 0.125)
        if i == order[min(1, nc - 1)]:
            start(0, 1)
    start(0, 2)
    start(0, 3)

    row = iota((ny, nz), 0)
    lane = iota((ny, nz), 1)
    for i in range(nl):
        inv_k[i] = jnp.exp(-dirs[0, i])
    for i in range(nl):
        k, scale, storage = level(i)
        own = inv_k[i]
        along_y = jnp.where(row < ny - k, 2.0 * scale / (own + roll(own, -k, 0)), 0.0)
        along_z = jnp.where(lane < nz - k, 2.0 * scale / (own + roll(own, -k, 1)), 0.0)
        t_y[i] = along_y
        t_z[i] = along_z
        inv_d[i] = storage + (along_y + roll(along_y, k, 0)) + (along_z + roll(along_z, k, 1))
    for i in range(nl):
        if i not in (nx - 1, nl - 1):
            along_x = 2.0 * level(i)[1] / (inv_k[i] + inv_k[i + 1])
            t_x[i] = along_x
            inv_d[i] += along_x
            inv_d[i + 1] += along_x

    src_in.wait()
    for i in range(nl):
        if i < nx:
            res[i] = src_ref[i]
        else:
            j = 2 * (i - nx)
            res[i] = pooled(src_ref[j], src_ref[j + 1])

    low = jnp.full((1, nz), low_ref[0])
    high = jnp.full((1, nz), high_ref[0])
    theta = (high + low) * 0.5
    delta = (high - low) * 0.5
    sigma = theta / delta
    rho = 1.0 / sigma

    flag = {axis: tuple(h.astype(jnp.float32) for h in has[axis]) for axis in AXES}
    row_b = iota((ROWS, nz), 0)
    lane_b = iota((ny, LANES), 1)
    tile_y = (slice(0, ROWS), slice(ny - ROWS, ny))
    tile_z = (slice(0, LANES), slice(nz - LANES, nz))

    def side_x(turn, side, lev):
        return halo_x[turn, side] if lev == 0 else unpacked(halo_c[turn, side])

    def side_y(turn, side, i):
        return halo_y[turn, side, i:i + 1, :]

    def side_z(turn, side, i):
        k = level(i)[0]
        return roll(halo_z[turn, side, i], k if side == 0 else -k, 1)

    edge = {(0, 0): 0, (0, 1): nx - 1, (1, 0): nx, (1, 1): nl - 1}

    arrive(0, 3)
    for i in range(nl):
        k, scale, _ = level(i)
        for side in (0, 1):
            at = lane_b < k if side == 0 else lane_b >= LANES - k
            beyond = jnp.exp(-side_z(0, side, i))
            t = jnp.where(at, 2.0 * scale / (inv_k[i, :, tile_z[side]] + beyond), 0.0)
            t = t * flag["gz"][side]
            b_z[side, i] = t
            inv_d[i, :, tile_z[side]] += t
    arrive(0, 2)
    for i in range(nl):
        k, scale, _ = level(i)
        for side in (0, 1):
            at = row_b < k if side == 0 else row_b >= ROWS - k
            beyond = jnp.exp(-side_y(0, side, i))
            t = jnp.where(at, 2.0 * scale / (inv_k[i, tile_y[side], :] + beyond), 0.0)
            t = t * flag["gy"][side]
            b_y[side, i] = t
            inv_d[i, tile_y[side], :] += t
    arrive(0, 1)
    arrive(0, 0)
    for (lev, side), i in edge.items():
        t = 2.0 * level(i)[1] / (inv_k[i] + jnp.exp(-side_x(0, side, lev))) * flag["gx"][side]
        b_x[lev, side] = t
        inv_d[i] += t

    inv_theta = 1.0 / theta
    for i in order:
        inverse = 1.0 / inv_d[i]
        inv_d[i] = inverse
        direction = res[i] * inverse * inv_theta
        put(1, i, direction)
        sol[i] = direction
    for turn in range(1, DEGREE + 1):
        for kind in (0, 1, 2, 3):
            start(turn, kind)
        for i in range(nl):
            k, _, storage = level(i)
            d = dirs[turn, i]
            flow_y = t_y[i] * (d - roll(d, -k, 0))
            flow_z = t_z[i] * (d - roll(d, -k, 1))
            r = res[i] - storage * d
            r = r - (flow_y - roll(flow_y, k, 0)) - (flow_z - roll(flow_z, k, 1))
            if i not in (0, nx):
                r = r + t_x[i - 1] * (dirs[turn, i - 1] - d)
            if i not in (nx - 1, nl - 1):
                r = r - t_x[i] * (d - dirs[turn, i + 1])
            res[i] = r
        arrive(turn, 3)
        for i in range(nl):
            for side in (0, 1):
                at = tile_z[side]
                res[i, :, at] -= b_z[side, i] * (dirs[turn, i, :, at] - side_z(turn, side, i))
        arrive(turn, 2)
        for i in range(nl):
            for side in (0, 1):
                at = tile_y[side]
                res[i, at, :] -= b_y[side, i] * (dirs[turn, i, at, :] - side_y(turn, side, i))
        arrive(turn, 1)
        arrive(turn, 0)
        for (lev, side), i in edge.items():
            res[i] -= b_x[lev, side] * (dirs[turn, i] - side_x(turn, side, lev))
        rho_next = 1.0 / (2.0 * sigma - rho)
        keep = rho_next * rho
        gain = 2.0 * rho_next / delta
        rho = rho_next
        for i in order:
            direction = keep * dirs[turn, i] + gain * (res[i] * inv_d[i])
            if turn < DEGREE:
                sol[i] += direction
                put(turn + 1, i, direction)
            elif i >= nx:
                sol[i] += direction
            else:
                total = sol[i] + direction
                fine_ref[i] = total
                diff_ref[i] = total - sol[nx + i // 2]

    fine_out = pltpu.make_async_copy(fine_ref, fine_hbm, io_sem.at[2])
    diff_out = pltpu.make_async_copy(diff_ref, diff_hbm, io_sem.at[3])
    fine_out.start()
    diff_out.start()
    for turn in range(DEGREE + 1):
        for kind in (0, 1, 2, 3):
            drain(turn, kind)
    fine_out.wait()
    diff_out.wait()


def shards(sizes, log_perm, source, low_bound, high_bound):
    nx, ny, nz = log_perm.shape
    nc = nx // 2
    nl = nx + nc
    pack = -(-nl // ROWS) * ROWS
    turns = DEGREE + 1
    f32 = lambda *shape: pltpu.VMEM(shape, jnp.float32)
    block = f32(nx, ny, nz)
    both = f32(nl, ny, nz)
    shape = jax.ShapeDtypeStruct((nx, ny, nz), jnp.float32)
    smem = pl.BlockSpec(memory_space=pltpu.SMEM)
    hbm = pl.BlockSpec(memory_space=pl.ANY)
    return pl.pallas_call(
        functools.partial(kernel, sizes),
        out_shape=(shape, shape),
        in_specs=[smem, smem, hbm, hbm],
        out_specs=(hbm, hbm),
        scratch_shapes=[
            block, block, block, block,
            f32(turns, nl, ny, nz),
            f32(turns, 2, ny // 2, nz // 2),
            f32(turns, 2, pack, nz),
            f32(turns, 2, ny, nz),
            f32(turns, 2, ny // 2, nz // 2),
            f32(turns, 2, pack, nz),
            f32(turns, 2, nl, ny, LANES),
            both, both, both, both,
            f32(2, 2, ny, nz),
            f32(2, nl, ROWS, nz),
            f32(2, nl, ny, LANES),
            both, both, both,
            pltpu.SemaphoreType.DMA((4,)),
            pltpu.SemaphoreType.DMA((turns, 4, 2)),
            pltpu.SemaphoreType.DMA((turns, 4, 2)),
        ],
        compiler_params=pltpu.CompilerParams(collective_id=0, has_side_effects=True),
    )(low_bound, high_bound, log_perm, source)


def solution(mesh):
    sizes = {axis: mesh.shape[axis] for axis in AXES}
    spec = P(("groups", "gx"), "gy", "gz")
    return jax.shard_map(
        functools.partial(shards, sizes),
        mesh=mesh,
        in_specs=(spec, spec, P(), P()),
        out_specs=(spec, spec),
        check_vma=False,
    )
```

time: 143 us -> 22.5 us (0.16); the launches traced: 140 us -> 22.3 us
  starting transfers between devices: 76.8 us -> 0 us
  local copies, waits for them, and re-layouts: 31.7 us -> 2.26 us
  Pallas kernels: 0 us -> 18.1 us
  other arithmetic: 16.5 us -> 0 us
  waiting for transfers between devices: 12.5 us -> 0 us
    ppermute x30 -> x0, starting transfers between devices: 76.8 us -> none  [the longest x15 57.5 us: extended_2(): before = lax.ppermute(last, axis, up)]
    reshape x3 -> x0, local copies, waits for them, and re-layouts: 27.3 us -> none  [the longest x1 10.5 us: shards(): coarse_perm = jnp.exp(log_perm.reshape(blocks).mean(axis=(1, 3, 5)))]
    pallas_call x0 -> x1, Pallas kernels: none -> 18.1 us  [shards(): pl.pallas_call(functools.partial(kernel, sizes), out_shape=(shape, shape)...]
    ppermute x30 -> x0, waiting for transfers between devices: 12.5 us -> none  [the longest x15 9.02 us: extended_2(): before = lax.ppermute(last, axis, up)]
    reduce_sum x2 -> x0, other arithmetic: 8.11 us -> none  [the longest x1 4.06 us: shards(): coarse_perm = jnp.exp(log_perm.reshape(blocks).mean(axis=(1, 3, 5)))]
    add x5 -> x0, other arithmetic: 4.14 us -> none  [the longest x2 3.83 us: fine_deep(): rho_next * rho_now * crop_one(direction)]
    broadcast_in_dim x1 -> x0, local copies, waits for them, and re-layouts: 3.84 us -> none  [refine(): jnp.broadcast_to(field[:, None, :, None, :, None], (size_x, 2, size_y, 2,...]
    unnamed x4, local copies, waits for them, and re-layouts: 0.01 us -> 2.26 us
  transfers between devices with their start and end apart: 30 -> 0, of which waited for: 10 -> 0; matrix products, arithmetic and copies ran while one was open for 18% -> 0% of each run, Pallas kernels for 0% -> 0%
where the time goes in v1:
time: 22.5 us; the launch traced here: 22.3 us
  Pallas kernels  18.1 us (80%)
  local copies, waits for them, and re-layouts  2.26 us (10%)
  between operations  1.94 us (9%)
    pallas_call x1, Pallas kernels, shards(): pl.pallas_call(functools.partial(kernel, sizes), out_shape=(shape, shape)...  18.1 us
    unnamed x4, local copies, waits for them, and re-layouts  2.26 us

profile of v1, /device:TPU:0, one launch (start us, length us, event | category | flops | bytes accessed | tf_op | source)
XLA Modules:
  0.0 22.3 jit_solution(13262422112106718251)
XLA Ops:
  1.9 18.1 %shard_map.59 = (f32[4,16,512]{2,1,0:T(8,128)}, f32[4,16,512]{2,1,0:T(8,128)}) custom-call(f32[1]{0:T(128)S(6)} %copy.8.low_ref, f32[1]{0:T(128)S(6)} %copy.9.high_ref, f32[4,16,512]{2,1,0:T(8,128)} %log_hbm.1, f32[4,16,512]{2,1,0:T(8,128)} %src_hbm.1), custom_call_target="tpu_custom_call" | custom-call | tf_op jit(solution)/shard_map/pallas_call | solution.py:317
  20.1 0.0 copy-start
  20.1 1.6 %copy.10 = f32[4,16,512]{2,1,0:T(8,128)} copy(f32[4,16,512]{2,1,0:T(8,128)} %get-tuple-element.4) | data formatting | bytes 262144
  21.7 0.0 copy-done
  21.7 0.7 %copy.11 = f32[4,16,512]{2,1,0:T(8,128)} copy(f32[4,16,512]{2,1,0:T(8,128)S(1)} %copy-done) | data formatting | bytes 262144
Async XLA Ops:
  20.1 1.6 %copy-start = (f32[4,16,512]{2,1,0:T(8,128)S(1)}, f32[4,16,512]{2,1,0:T(8,128)}, u32[]{:S(2)}) copy-start(f32[4,16,512]{2,1,0:T(8,128)} %get-tuple-element.5) | copy-start | bytes 393220

commit v2 on v1

v2 whole, which is shorter than its diff:
```python
import functools

import jax
import jax.numpy as jnp
from jax import lax
from jax.experimental import pallas as pl
from jax.experimental.pallas import tpu as pltpu
from jax.sharding import PartitionSpec as P

DEGREE = 3
STORAGE = 0.1
LANES = 128
ROWS = 8
MESH = pl.DeviceIdType.MESH
AXES = ("gx", "gy", "gz")


def roll(a, shift, axis):
    return pltpu.roll(a, shift % a.shape[axis], axis)


def iota(shape, axis):
    return lax.broadcasted_iota(jnp.int32, shape, axis)


def even(shape, axis):
    return iota(shape, axis) % 2 == 0


def pair_sum(a, axis):
    return a + jnp.where(even(a.shape, axis), roll(a, -1, axis), roll(a, 1, axis))


def pooled(a, b):
    return pair_sum(pair_sum(a + b, 0), 1)


def packed(a):
    rows, lanes = a.shape[0] // 2, a.shape[1] // 2
    a = jnp.where(even((a.shape[0], lanes), 1), a[:, :lanes], a[:, lanes:])
    return jnp.where(even((rows, lanes), 0), a[:rows], a[rows:])


def unpacked(a):
    for axis in (0, 1):
        is_even = even(a.shape, axis)
        first = jnp.where(is_even, a, roll(a, 1, axis))
        second = jnp.where(is_even, roll(a, -1, axis), a)
        a = jnp.concatenate([first, second], axis=axis)
    return a


def kernel(sizes, low_ref, high_ref, log_hbm, src_hbm, sol, last,
           log_ref, src_ref, dirs, face_c, face_y, halo_x, halo_c, halo_y, halo_z,
           inv_k, t_x, t_y, t_z, b_x, b_y, b_z, held, inv_d, res,
           io_sem, send_sem, recv_sem):
    nx, ny, nz = log_ref.shape
    nc = nx // 2
    nl = nx + nc
    me = {axis: lax.axis_index(axis) for axis in AXES}
    has = {axis: (me[axis] > 0, me[axis] < sizes[axis] - 1) for axis in AXES}

    log_in = pltpu.make_async_copy(log_hbm, log_ref, io_sem.at[0])
    src_in = pltpu.make_async_copy(src_hbm, src_ref, io_sem.at[1])
    log_in.start()
    src_in.start()

    for axis, halos in (("gx", (halo_x, halo_c)), ("gy", (halo_y,)), ("gz", (halo_z,))):
        if sizes[axis] > 2:
            for halo in halos:
                halo[...] = jnp.zeros_like(halo)

    barrier = pltpu.get_barrier_semaphore()
    count = 0
    for axis in AXES:
        for side, step in ((0, -1), (1, 1)):
            if sizes[axis] > 1:
                @pl.when(has[axis][side])
                def _():
                    pl.semaphore_signal(barrier, inc=1, device_id={axis: me[axis] + step},
                                        device_id_type=MESH)
            count = count + has[axis][side].astype(jnp.int32)

    def sides(axis):
        if sizes[axis] == 1:
            return []
        if sizes[axis] == 2:
            return [(0, 1 - me[axis], None)]
        return [(s, s, has[axis][s].astype(jnp.float32)) for s in (0, 1)]

    def tile(side, length, size):
        first = side * (length - size)
        return pl.ds(first if isinstance(first, int) else pl.multiple_of(first, size), size)

    def faces(turn, kind):
        if kind == 0:
            source = log_hbm if turn == 0 else dirs.at[turn]
            return "gx", (lambda s: source.at[s * (nx - 1)]), (lambda s: halo_x.at[turn, s])
        if kind == 1:
            return "gx", (lambda s: face_c.at[turn, s]), (lambda s: halo_c.at[turn, s])
        if kind == 2:
            return "gy", (lambda s: face_y.at[turn, s]), (lambda s: halo_y.at[turn, s])
        return ("gz", (lambda s: dirs.at[turn, :, :, tile(s, nz, LANES)]),
                (lambda s: halo_z.at[turn, s]))

    def each(turn, kind, outgoing, act):
        axis, source_of, target_of = faces(turn, kind)
        n, here = sizes[axis], me[axis]
        if n == 1:
            return
        if n == 2:
            act(pltpu.make_async_remote_copy(
                src_ref=source_of(1 - here), dst_ref=target_of(here),
                send_sem=send_sem.at[turn, kind, 0], recv_sem=recv_sem.at[turn, kind, 0],
                device_id={axis: 1 - here}, device_id_type=MESH))
            return
        for side, step in ((0, -1), (1, 1)):
            there = 1 - side if outgoing else side

            @pl.when(has[axis][side])
            def _():
                act(pltpu.make_async_remote_copy(
                    src_ref=source_of(side), dst_ref=target_of(there),
                    send_sem=send_sem.at[turn, kind, side],
                    recv_sem=recv_sem.at[turn, kind, there],
                    device_id={axis: here + step}, device_id_type=MESH))

    def start(turn, kind):
        each(turn, kind, True, lambda copy: copy.start())

    def arrive(turn, kind):
        each(turn, kind, False, lambda copy: copy.wait_recv())

    def drain(turn, kind):
        each(turn, kind, True, lambda copy: copy.wait_send())

    def field(turn):
        return dirs.at[turn] if turn <= DEGREE else last

    def level(i):
        return (1, 1.0, STORAGE) if i < nx else (2, 2.0, 8.0 * STORAGE)

    def send_coarse(turn):
        face_c[turn, 0] = packed(dirs[turn, nx])
        face_c[turn, 1] = packed(dirs[turn, nl - 1])
        start(turn, 1)

    def send_rows(turn):
        for i in range(nl):
            face_y[turn, 0, i:i + 1, :] = dirs[turn, i, 0:1, :]
            face_y[turn, 1, i:i + 1, :] = dirs[turn, i, ny - 1:ny, :]
        start(turn, 2)

    log_in.wait()
    for i in range(nx):
        dirs[0, i] = log_ref[i]
    for j in range(nc):
        dirs[0, nx + j] = pooled(log_ref[2 * j], log_ref[2 * j + 1]) * 0.125
    pl.semaphore_wait(barrier, count)
    start(0, 0)
    send_coarse(0)
    send_rows(0)
    start(0, 3)

    row = iota((ny, nz), 0)
    lane = iota((ny, nz), 1)
    for i in range(nl):
        inv_k[i] = jnp.exp(-dirs[0, i])
    for i in range(nl):
        k, scale, storage = level(i)
        own = inv_k[i]
        along_y = jnp.where(row < ny - k, 2.0 * scale / (own + roll(own, -k, 0)), 0.0)
        along_z = jnp.where(lane < nz - k, 2.0 * scale / (own + roll(own, -k, 1)), 0.0)
        t_y[i] = along_y
        t_z[i] = along_z
        inv_d[i] = (along_y + roll(along_y, k, 0)) + (along_z + roll(along_z, k, 1))
        held[i] = jnp.full((ny, nz), storage)
    for i in range(nl):
        if i not in (nx - 1, nl - 1):
            along_x = 2.0 * level(i)[1] / (inv_k[i] + inv_k[i + 1])
            t_x[i] = along_x
            inv_d[i] += along_x
            inv_d[i + 1] += along_x

    src_in.wait()
    for i in range(nx):
        res[i] = src_ref[i]
    for j in range(nc):
        res[nx + j] = pooled(src_ref[2 * j], src_ref[2 * j + 1])

    low = jnp.full((1, nz), low_ref[0])
    high = jnp.full((1, nz), high_ref[0])
    theta = (high + low) * 0.5
    delta = (high - low) * 0.5
    sigma = theta / delta
    rho = 1.0 / sigma
    inv_theta = 1.0 / theta

    row_b = iota((ROWS, nz), 0)
    lane_b = iota((ny, LANES), 1)

    def beside(index, side, size, k):
        first = side * (size - k)
        return (index >= first) & (index < first + k)

    def side_x(turn, side, lev):
        return halo_x[turn, side] if lev == 0 else unpacked(halo_c[turn, side])

    def side_y(turn, side, i):
        return halo_y[turn, side, i:i + 1, :]

    def side_z(turn, side, i):
        k = level(i)[0]
        return pltpu.roll(halo_z[turn, side, i], k + side * (LANES - 2 * k), 1)

    def edge(lev, side):
        if isinstance(side, int):
            return (0, nx - 1)[side] if lev == 0 else (nx, nl - 1)[side]
        return side * (nx - 1) if lev == 0 else nx + side * (nc - 1)

    def across(at, scale, own, beyond, factor):
        t = 2.0 * scale / (own + jnp.exp(-beyond))
        if at is not None:
            t = jnp.where(at, t, 0.0)
        return t if factor is None else t * factor

    arrive(0, 3)
    for slot, side, factor in sides("gz"):
        where = tile(side, nz, LANES)
        for i in range(nl):
            k, scale, _ = level(i)
            t = across(beside(lane_b, side, LANES, k), scale, inv_k[i, :, where],
                       side_z(0, side, i), factor)
            b_z[slot, i] = t
            held[i, :, where] += t
    arrive(0, 2)
    for slot, side, factor in sides("gy"):
        where = tile(side, ny, ROWS)
        for i in range(nl):
            k, scale, _ = level(i)
            t = across(beside(row_b, side, ROWS, k), scale, inv_k[i, where, :],
                       side_y(0, side, i), factor)
            b_y[slot, i] = t
            held[i, where, :] += t

    def begin(i):
        inverse = 1.0 / (inv_d[i] + held[i])
        inv_d[i] = inverse
        dirs[1, i] = res[i] * inverse * inv_theta

    for i in range(1, nx - 1):
        begin(i)
    for lev in (0, 1):
        arrive(0, lev)
        for slot, side, factor in sides("gx"):
            i = edge(lev, side)
            t = across(None, (1.0, 2.0)[lev], inv_k[i], side_x(0, side, lev), factor)
            b_x[lev, slot] = t
            held[i] += t
        if lev == 0:
            for i in dict.fromkeys((0, nx - 1)):
                begin(i)
            start(1, 0)
    for i in range(nx, nl):
        begin(i)
    send_coarse(1)
    send_rows(1)
    start(1, 3)

    for turn in range(1, DEGREE + 1):
        rho_next = 1.0 / (2.0 * sigma - rho)
        keep = rho_next * rho
        gain = 2.0 * rho_next / delta
        rho = rho_next
        later = field(turn + 1)
        flow_x = None
        for i in range(nl):
            k = level(i)[0]
            d = dirs[turn, i]
            sol[i] = d if turn == 1 else sol[i] + d
            flow_y = t_y[i] * (d - roll(d, -k, 0))
            flow_z = t_z[i] * (d - roll(d, -k, 1))
            r = res[i] - held[i] * d
            r = r - (flow_y - roll(flow_y, k, 0)) - (flow_z - roll(flow_z, k, 1))
            if i not in (0, nx):
                r = r + flow_x
            if i not in (nx - 1, nl - 1):
                flow_x = t_x[i] * (d - dirs[turn, i + 1])
                r = r - flow_x
            res[i] = r
            later[i] = keep * d + gain * (r * inv_d[i])

        def add(at, t, wide):
            if turn < DEGREE:
                res[at] += t
            later[at] += wide * (t * inv_d[at])

        arrive(turn, 3)
        for slot, side, _ in sides("gz"):
            for i in range(nl):
                add((i, slice(None), tile(side, nz, LANES)),
                    b_z[slot, i] * side_z(turn, side, i), gain[:, :LANES])
        arrive(turn, 2)
        for slot, side, _ in sides("gy"):
            for i in range(nl):
                add((i, tile(side, ny, ROWS), slice(None)),
                    b_y[slot, i] * side_y(turn, side, i), gain)
        for lev in (0, 1):
            arrive(turn, lev)
            for slot, side, _ in sides("gx"):
                add((edge(lev, side),), b_x[lev, slot] * side_x(turn, side, lev), gain)
            if lev == 0 and turn < DEGREE:
                start(turn + 1, 0)
        if turn < DEGREE:
            send_coarse(turn + 1)
            send_rows(turn + 1)
            start(turn + 1, 3)

    for turn in range(DEGREE + 1):
        for kind in (0, 1, 2, 3):
            drain(turn, kind)


def shards(sizes, log_perm, source, low_bound, high_bound):
    nx, ny, nz = log_perm.shape
    nc = nx // 2
    nl = nx + nc
    pack = -(-nl // ROWS) * ROWS
    turns = DEGREE + 1
    f32 = lambda *shape: pltpu.VMEM(shape, jnp.float32)
    block = f32(nx, ny, nz)
    both = f32(nl, ny, nz)
    shape = jax.ShapeDtypeStruct((nl, ny, nz), jnp.float32)
    smem = pl.BlockSpec(memory_space=pltpu.SMEM)
    hbm = pl.BlockSpec(memory_space=pl.ANY)
    vmem = pl.BlockSpec(memory_space=pltpu.VMEM)
    sol, last = pl.pallas_call(
        functools.partial(kernel, sizes),
        out_shape=(shape, shape),
        in_specs=[smem, smem, hbm, hbm],
        out_specs=(vmem, vmem),
        scratch_shapes=[
            block, block,
            f32(turns, nl, ny, nz),
            f32(turns, 2, ny // 2, nz // 2),
            f32(turns, 2, pack, nz),
            f32(turns, 2, ny, nz),
            f32(turns, 2, ny // 2, nz // 2),
            f32(turns, 2, pack, nz),
            f32(turns, 2, nl, ny, LANES),
            both, both, both, both,
            f32(2, 2, ny, nz),
            f32(2, nl, ROWS, nz),
            f32(2, nl, ny, LANES),
            both, both, both,
            pltpu.SemaphoreType.DMA((2,)),
            pltpu.SemaphoreType.DMA((turns, 4, 2)),
            pltpu.SemaphoreType.DMA((turns, 4, 2)),
        ],
        compiler_params=pltpu.CompilerParams(
            collective_id=0, has_side_effects=True, vmem_limit_bytes=16 * 2**20),
    )(low_bound, high_bound, log_perm, source)
    total = sol + last
    fine = total[:nx]
    return fine, fine - jnp.repeat(total[nx:], 2, axis=0)


def solution(mesh):
    sizes = {axis: mesh.shape[axis] for axis in AXES}
    spec = P(("groups", "gx"), "gy", "gz")
    return jax.shard_map(
        functools.partial(shards, sizes),
        mesh=mesh,
        in_specs=(spec, spec, P(), P()),
        out_specs=(spec, spec),
        check_vma=False,
    )
```

time: 22.5 us -> 21.7 us (0.964)
  Pallas kernels: 18.1 us -> 17 us
  other arithmetic: 0 us -> 0.75 us
  local copies, waits for them, and re-layouts: 2.26 us -> 1.81 us
    pallas_call x1, Pallas kernels: 18.1 us -> 17 us  [shards(): pl.pallas_call(functools.partial(kernel, sizes), out_shape=(shape, shape)...]
    sub x0 -> x1, other arithmetic: none -> 0.72 us  [shards(): return (fine, fine - jnp.repeat(total[nx:], 2, axis=0))]
    unnamed x4, local copies, waits for them, and re-layouts: 2.26 us -> 1.8 us
where the time goes in v2:
time: 21.7 us; the launch traced here: 21.6 us
  Pallas kernels  17 us (78%)
  between operations  1.95 us (9%)
  local copies, waits for them, and re-layouts  1.81 us (8%)
  other arithmetic  0.75 us (3%)
    pallas_call x1, Pallas kernels, shards(): pl.pallas_call(functools.partial(kernel, sizes), out_shape=(shape, shape)...  17 us
    unnamed x4, local copies, waits for them, and re-layouts  1.8 us
    sub x1, other arithmetic, shards(): return (fine, fine - jnp.repeat(total[nx:], 2, axis=0))  0.72 us

profile of v2, /device:TPU:0, one launch (start us, length us, event | category | flops | bytes accessed | tf_op | source)
XLA Modules:
  0.0 21.6 jit_solution(6293736954499671208)
XLA Ops:
  1.9 0.0 copy-start
  1.9 0.9 %copy-done = f32[4,16,512]{2,1,0:T(8,128)S(1)} copy-done((f32[4,16,512]{2,1,0:T(8,128)S(1)}, f32[4,16,512]{2,1,0:T(8,128)}, u32[]{:S(2)}) %copy-start) | copy-done | bytes 131096
  2.8 0.0 copy-start.1
  2.8 0.9 %copy-done.1 = f32[4,16,512]{2,1,0:T(8,128)S(1)} copy-done((f32[4,16,512]{2,1,0:T(8,128)S(1)}, f32[4,16,512]{2,1,0:T(8,128)}, u32[]{:S(2)}) %copy-start.1) | copy-done | bytes 131096
  3.7 17.0 %shard_map.59 = (f32[6,16,512]{2,1,0:T(8,128)S(1)}, f32[6,16,512]{2,1,0:T(8,128)S(1)}) custom-call(f32[1]{0:T(128)S(6)} %copy.6.low_ref, f32[1]{0:T(128)S(6)} %copy.7.high_ref, f32[4,16,512]{2,1,0:T(8,128)S(1)} %copy-done, f32[4,16,512]{2,1,0:T(8,128)S(1)} %copy-done.1), custom_call_target="tpu_custom_call" | custom-call | tf_op jit(solution)/shard_map/pallas_call | solution.py:337
  20.8 0.7 %bitcast_subtract_fusion = (f32[4,16,512]{2,1,0:T(8,128)}, f32[4,16,512]{2,1,0:T(8,128)}) fusion(f32[2,16,512]{2,1,0:T(8,128)S(1)} %slice.9, f32[6,16,512]{2,1,0:T(8,128)S(1)} %add.3), kind=kLoop, calls=%fused_computation | loop fusion | flops 32768 | bytes 458752 | tf_op jit(solution)/shard_map/sub | solution.py:365
  (2 shorter events, 0.0 us)
Async XLA Ops:
  1.9 0.9 %copy-start = (f32[4,16,512]{2,1,0:T(8,128)S(1)}, f32[4,16,512]{2,1,0:T(8,128)}, u32[]{:S(2)}) copy-start(f32[4,16,512]{2,1,0:T(8,128)} %log_hbm.1) | copy-start | bytes 393220
  2.8 0.9 %copy-start.1 = (f32[4,16,512]{2,1,0:T(8,128)S(1)}, f32[4,16,512]{2,1,0:T(8,128)}, u32[]{:S(2)}) copy-start(f32[4,16,512]{2,1,0:T(8,128)} %src_hbm.1) | copy-start | bytes 393220

commit v3 on v2

--- a/solution.py
+++ b/solution.py
@@ -50,8 +50,8 @@
     return a
 
 
-def kernel(sizes, low_ref, high_ref, log_hbm, src_hbm, sol, last,
-           log_ref, src_ref, dirs, face_c, face_y, halo_x, halo_c, halo_y, halo_z,
+def kernel(sizes, low_hbm, high_hbm, log_hbm, src_hbm, sol, last,
+           low_ref, high_ref, log_ref, src_ref, dirs, face_c, face_y, halo_x, halo_c, halo_y, halo_z,
            inv_k, t_x, t_y, t_z, b_x, b_y, b_z, held, inv_d, res,
            io_sem, send_sem, recv_sem):
     nx, ny, nz = log_ref.shape
@@ -60,26 +60,36 @@
     me = {axis: lax.axis_index(axis) for axis in AXES}
     has = {axis: (me[axis] > 0, me[axis] < sizes[axis] - 1) for axis in AXES}
 
-    log_in = pltpu.make_async_copy(log_hbm, log_ref, io_sem.at[0])
-    src_in = pltpu.make_async_copy(src_hbm, src_ref, io_sem.at[1])
-    log_in.start()
-    src_in.start()
-
-    for axis, halos in (("gx", (halo_x, halo_c)), ("gy", (halo_y,)), ("gz", (halo_z,))):
-        if sizes[axis] > 2:
-            for halo in halos:
-                halo[...] = jnp.zeros_like(halo)
-
     barrier = pltpu.get_barrier_semaphore()
     count = 0
     for axis in AXES:
-        for side, step in ((0, -1), (1, 1)):
-            if sizes[axis] > 1:
+        if sizes[axis] == 2:
+            pl.semaphore_signal(barrier, inc=1, device_id={axis: 1 - me[axis]},
+                                device_id_type=MESH)
+            count = count + 1
+        elif sizes[axis] > 2:
+            for side, step in ((0, -1), (1, 1)):
                 @pl.when(has[axis][side])
                 def _():
                     pl.semaphore_signal(barrier, inc=1, device_id={axis: me[axis] + step},
                                         device_id_type=MESH)
-            count = count + has[axis][side].astype(jnp.int32)
+                count = count + has[axis][side].astype(jnp.int32)
+
+    log_in = pltpu.make_async_copy(log_hbm, log_ref, io_sem.at[0])
+    src_in = pltpu.make_async_copy(src_hbm, src_ref, io_sem.at[1])
+    low_in = pltpu.make_async_copy(low_hbm, low_ref, io_sem.at[2])
+    high_in = pltpu.make_async_copy(high_hbm, high_ref, io_sem.at[3])
+    for copy in (log_in, src_in, low_in, high_in):
+        copy.start()
+
+    for axis, halos in (("gx", (halo_x, halo_c)), ("gy", (halo_y,)), ("gz", (halo_z,))):
+        if sizes[axis] > 2:
+            for side in (0, 1):
+                @pl.when(jnp.logical_not(has[axis][side]))
+                def _():
+                    for halo in halos:
+                        for turn in range(DEGREE + 1):
+                            halo[turn, side] = jnp.zeros_like(halo[turn, side])
 
     def sides(axis):
         if sizes[axis] == 1:
@@ -182,7 +192,8 @@
             inv_d[i] += along_x
             inv_d[i + 1] += along_x
 
-    src_in.wait()
+    for copy in (src_in, low_in, high_in):
+        copy.wait()
     for i in range(nx):
         res[i] = src_ref[i]
     for j in range(nc):
@@ -273,6 +284,8 @@
         gain = 2.0 * rho_next / delta
         rho = rho_next
         later = field(turn + 1)
+        for kind in (0, 1, 2, 3):
+            drain(turn - 1, kind)
         flow_x = None
         for i in range(nl):
             k = level(i)[0]
@@ -316,9 +329,8 @@
             send_rows(turn + 1)
             start(turn + 1, 3)
 
-    for turn in range(DEGREE + 1):
-        for kind in (0, 1, 2, 3):
-            drain(turn, kind)
+    for kind in (0, 1, 2, 3):
+        drain(DEGREE, kind)
 
 
 def shards(sizes, log_perm, source, low_bound, high_bound):
@@ -331,15 +343,16 @@
     block = f32(nx, ny, nz)
     both = f32(nl, ny, nz)
     shape = jax.ShapeDtypeStruct((nl, ny, nz), jnp.float32)
-    smem = pl.BlockSpec(memory_space=pltpu.SMEM)
-    hbm = pl.BlockSpec(memory_space=pl.ANY)
+    hbm = pl.BlockSpec(memory_space=pltpu.HBM)
     vmem = pl.BlockSpec(memory_space=pltpu.VMEM)
     sol, last = pl.pallas_call(
         functools.partial(kernel, sizes),
         out_shape=(shape, shape),
-        in_specs=[smem, smem, hbm, hbm],
+        in_specs=[hbm] * 4,
         out_specs=(vmem, vmem),
         scratch_shapes=[
+            pltpu.SMEM((1,), jnp.float32),
+            pltpu.SMEM((1,), jnp.float32),
             block, block,
             f32(turns, nl, ny, nz),
             f32(turns, 2, ny // 2, nz // 2),
@@ -353,7 +366,7 @@
             f32(2, nl, ROWS, nz),
             f32(2, nl, ny, LANES),
             both, both, both,
-            pltpu.SemaphoreType.DMA((2,)),
+            pltpu.SemaphoreType.DMA((4,)),
             pltpu.SemaphoreType.DMA((turns, 4, 2)),
             pltpu.SemaphoreType.DMA((turns, 4, 2)),
         ],

time: 21.7 us -> 21.4 us (0.986)
  Pallas kernels: 17 us -> 16.7 us
    pallas_call x1, Pallas kernels: 17 us -> 16.7 us  [shards(): pl.pallas_call(functools.partial(kernel, sizes), out_shape=(shape, shape)...]
where the time goes in v3:
time: 21.4 us; the launch traced here: 21.2 us
  Pallas kernels  16.7 us (78%)
  between operations  1.95 us (9%)
  local copies, waits for them, and re-layouts  1.81 us (8%)
  other arithmetic  0.75 us (4%)
    pallas_call x1, Pallas kernels, shards(): pl.pallas_call(functools.partial(kernel, sizes), out_shape=(shape, shape)...  16.7 us
    unnamed x4, local copies, waits for them, and re-layouts  1.8 us
    sub x1, other arithmetic, shards(): return (fine, fine - jnp.repeat(total[nx:], 2, axis=0))  0.72 us

profile of v3, /device:TPU:0, one launch (start us, length us, event | category | flops | bytes accessed | tf_op | source)
XLA Modules:
  0.0 21.2 jit_solution(10014483492839351564)
XLA Ops:
  1.9 0.0 copy-start
  1.9 0.9 %copy-done = f32[4,16,512]{2,1,0:T(8,128)S(1)} copy-done((f32[4,16,512]{2,1,0:T(8,128)S(1)}, f32[4,16,512]{2,1,0:T(8,128)}, u32[]{:S(2)}) %copy-start) | copy-done | bytes 131096
  2.8 0.0 copy-start.1
  2.8 0.9 %copy-done.1 = f32[4,16,512]{2,1,0:T(8,128)S(1)} copy-done((f32[4,16,512]{2,1,0:T(8,128)S(1)}, f32[4,16,512]{2,1,0:T(8,128)}, u32[]{:S(2)}) %copy-start.1) | copy-done | bytes 131096
  3.7 16.7 %shard_map.59 = (f32[6,16,512]{2,1,0:T(8,128)S(1)}, f32[6,16,512]{2,1,0:T(8,128)S(1)}) custom-call(f32[1]{0:T(128)S(6)} %copy.6.low_hbm, f32[1]{0:T(128)S(6)} %copy.7.high_hbm, f32[4,16,512]{2,1,0:T(8,128)S(1)} %copy-done, f32[4,16,512]{2,1,0:T(8,128)S(1)} %copy-done.1), custom_call_target="tpu_custom_call" | custom-call | tf_op jit(solution)/shard_map/pallas_call | solution.py:348
  20.5 0.7 %bitcast_subtract_fusion = (f32[4,16,512]{2,1,0:T(8,128)}, f32[4,16,512]{2,1,0:T(8,128)}) fusion(f32[2,16,512]{2,1,0:T(8,128)S(1)} %slice.9, f32[6,16,512]{2,1,0:T(8,128)S(1)} %add.3), kind=kLoop, calls=%fused_computation | loop fusion | flops 32768 | bytes 458752 | tf_op jit(solution)/shard_map/sub | solution.py:378
  (2 shorter events, 0.0 us)
Async XLA Ops:
  1.9 0.9 %copy-start = (f32[4,16,512]{2,1,0:T(8,128)S(1)}, f32[4,16,512]{2,1,0:T(8,128)}, u32[]{:S(2)}) copy-start(f32[4,16,512]{2,1,0:T(8,128)} %log_hbm.1) | copy-start | bytes 393220
  2.8 0.9 %copy-start.1 = (f32[4,16,512]{2,1,0:T(8,128)S(1)}, f32[4,16,512]{2,1,0:T(8,128)}, u32[]{:S(2)}) copy-start(f32[4,16,512]{2,1,0:T(8,128)} %src_hbm.1) | copy-start | bytes 393220
